TPU v7x, 256 devices: a whole 4x4x8 slice. The times are simulated.
256 devices in a mesh: proj: 64 (over y, z, core), grp: 4 (over x).
Axes of the slice: x: 4, y: 4, z: 8, core: 2. Of those that a mesh axis runs over, the one named last changes fastest.
Arguments:
- grads: bfloat16 [1024, 131072], P('grp', 'proj'), may hold values from -16 to 16
- proj_matrix: bfloat16 [131072, 8192], P('proj', 'grp'), may hold values from -48 to 48
- targets: bfloat16 [2048, 8192], P('proj', 'grp'), may hold values from -480 to 480
Outputs:
- scores: float32 [1024, 2048], P('proj', 'grp')
All inputs are finite; a program needn't handle non-finite values.
Results may differ from a plain program's by a relative error of at most 0.0029.
Values may be sent and summed in bfloat16 or wider, within the bound.
A program may use at most 128 MiB of HBM per device.

v0:
```python
import jax
import jax.numpy as jnp
from jax import lax
from jax.sharding import PartitionSpec as P

K = 8192


def inner_rows(left, right):
    return lax.dot_general(
        left, right, (((1,), (1,)), ((), ())), preferred_element_type=jnp.float32
    )


def per_device(grads, proj_matrix, targets):
    gathered = lax.all_gather(grads, "grp", axis=0, tiled=True)
    features = lax.psum_scatter(
        jnp.dot(gathered, proj_matrix, preferred_element_type=jnp.float32),
        "proj",
        scatter_dimension=0,
        tiled=True,
    )
    rounded = features.astype(jnp.bfloat16)
    feature_sq = jnp.sum(jnp.square(rounded.astype(jnp.float32)), axis=1)
    target_all = lax.all_gather(targets, "proj", axis=0, tiled=True)
    target_sq = jnp.sum(jnp.square(target_all.astype(jnp.float32)), axis=1)
    products = inner_rows(rounded, target_all)
    feature_sq, target_sq = lax.psum((feature_sq, target_sq), "grp")
    products = lax.psum_scatter(products, "grp", scatter_dimension=1, tiled=True)
    own_cols = products.shape[1]
    target_sq = lax.dynamic_slice_in_dim(target_sq, lax.axis_index("grp") * own_cols, own_cols, 0)
    factor = float(K) ** 0.5
    return (
        factor
        * products
        * lax.rsqrt(feature_sq + 1e-06)[:, None]
        * lax.rsqrt(target_sq + 1e-06)[None, :]
    )


def solution(mesh):
    placed = (P("grp", "proj"), P("proj", "grp"), P("proj", "grp"))
    return jax.shard_map(
        per_device, mesh=mesh, in_specs=placed, out_specs=P("proj", "grp"), check_vma=False
    )
```

profile of v0, /device:TPU:1, one launch (start us, length us, event | category | flops | bytes accessed | tf_op | source)
XLA Modules:
  0.0 336.1 jit_solution(5855670005372948281)
XLA Ops:
  6.5 0.0 all-gather.3.cloned.1.call-start
  6.5 0.7 all-gather.3.cloned.1.call-update
  7.3 0.0 all-gather.5.cloned.1.call-start
  7.3 0.7 all-gather.5.cloned.1.call-update
  8.0 0.0 reduce-scatter.3.cloned.1.call-start
  8.1 55.7 %all-gather.3.cloned.1.call-done = bf16[1024,2048]{1,0:T(8,128)(2,1)} async-done(((bf16[256,2048]{1,0:T(8,128)(2,1)}), bf16[1024,2048]{1,0:T(8,128)(2,1)}) %all-gather.3.cloned.1.call-update) | async-done | bytes 4194320 | tf_op jit(solution)/shard_map/all_gather | solution.py:16
  63.8 14.4 %fusion.2 = f32[1024,2048]{1,0:T(8,128)} fusion(bf16[1024,2048]{1,0:T(8,128)(2,1)} %all-gather.3.cloned.1.call-done, bf16[2048,2048]{1,0:T(8,128)(2,1)} %param.4), kind=kOutput, calls=%fused_computation.7 | convolution fusion | flops 8589934592 | bytes 20971520 | tf_op jit(solution)/shard_map/dot_general | solution.py:18
  78.2 0.0 reduce-scatter.3.cloned.1.call-update
  78.2 0.0 reduce-scatter.5.cloned.1.call-start
  78.3 72.2 %all-gather.5.cloned.1.call-done = bf16[2048,2048]{1,0:T(8,128)(2,1)} async-done(((bf16[32,2048]{1,0:T(8,128)(2,1)}), bf16[2048,2048]{1,0:T(8,128)(2,1)}) %all-gather.5.cloned.1.call-update) | async-done | bytes 8388624 | tf_op jit(solution)/shard_map/all_gather | solution.py:25
  150.5 5.1 %multiply_reduce_fusion = f32[2048]{0:T(1024)S(1)} fusion(bf16[2048,2048]{1,0:T(8,128)(2,1)} %all-gather.5.cloned.1.call-done), kind=kLoop, calls=%fused_computation | loop fusion | flops 12580864 | bytes 8396800 | tf_op jit(solution)/shard_map/reduce_sum | solution.py:26
  155.6 142.3 %reduce-scatter.3.cloned.1.call-done = f32[16,2048]{1,0:T(8,128)} async-done(((f32[1024,2048]{1,0:T(8,128)}), f32[16,2048]{1,0:T(8,128)}) %reduce-scatter.3.cloned.1.call-update) | async-done | bytes 131088 | tf_op jit(solution)/shard_map/reduce_scatter | solution.py:17
  297.9 0.0 copy-start
  297.9 6.4 %fusion = f32[16,2048]{1,0:T(8,128)} fusion(bf16[2048,2048]{1,0:T(8,128)(2,1)} %all-gather.5.cloned.1.call-done, f32[16,2048]{1,0:T(8,128)} %reduce-scatter.3.cloned.1.call-done), kind=kOutput, calls=%fused_computation.3 | convolution fusion | flops 134250496 | bytes 8650752 | tf_op jit(solution)/shard_map/dot_general | solution.py:10
  304.3 0.0 reduce-scatter.5.cloned.1.call-update
  304.3 0.0 copy-done
  304.4 0.1 multiply_reduce_fusion.1
  304.5 8.7 %all-reduce = (f32[2048]{0:T(1024)S(1)}, f32[16]{0:T(128)S(1)}) all-reduce(f32[2048]{0:T(1024)S(1)} %multiply_reduce_fusion, f32[16]{0:T(128)S(1)} %multiply_reduce_fusion.1), channel_id=1, replica_groups=mesh['proj'=64,'grp'=4] {'grp'}, use_global_device_ids=true, to_apply=%region_5.0 | all-reduce | flops 2064 | bytes 16512 | tf_op jit(solution)/shard_map/psum | solution.py:28
  313.2 0.1 add_rsqrt_fusion
  313.2 14.8 %reduce-scatter.5.cloned.1.call-done = f32[16,512]{1,0:T(8,128)} async-done(((f32[16,2048]{1,0:T(8,128)}), f32[16,512]{1,0:T(8,128)}) %reduce-scatter.5.cloned.1.call-update) | async-done | bytes 32784 | tf_op jit(solution)/shard_map/reduce_scatter | solution.py:29
  328.1 1.4 multiply_multiply_fusion
  (1 shorter events, 0.0 us)
Async XLA Ops:
  6.5 57.3 %all-gather.3.cloned.1.call-start = ((), (), s32[]{:S(2)}) async-start(), calls=%async_computation.2 | async-start | bytes 5242880 | tf_op jit(solution)/shard_map/all_gather | solution.py:16
  7.3 143.2 %all-gather.5.cloned.1.call-start = ((), (), s32[]{:S(2)}) async-start(), calls=%async_computation.4 | async-start | bytes 8519680 | tf_op jit(solution)/shard_map/all_gather | solution.py:25
  8.0 289.9 %reduce-scatter.3.cloned.1.call-start = ((), (), s32[]{:S(2)}) async-start(), calls=%async_computation.3 | async-start | bytes 8519680 | tf_op jit(solution)/shard_map/reduce_scatter | solution.py:17
  78.2 249.9 %reduce-scatter.5.cloned.1.call-start = ((), (), s32[]{:S(2)}) async-start(), calls=%async_computation.5 | async-start | bytes 163840 | tf_op jit(solution)/shard_map/reduce_scatter | solution.py:29
  297.9 6.5 %copy-start = (f32[16,2048]{1,0:T(8,128)S(1)}, f32[16,2048]{1,0:T(8,128)}, u32[]{:S(2)}) copy-start(f32[16,2048]{1,0:T(8,128)} %reduce-scatter.3.cloned.1.call-done) | copy-start | bytes 393220
Sparse Core Ops, SparseCore 0:
  9.2 54.5 all-gather.2
  66.6 83.8 all-gather.4
  154.7 143.1 reduce-scatter.2
  304.5 23.5 reduce-scatter.4
where the time goes:
time: 338 us; the launch traced here: 336 us
  waiting for transfers between devices  287 us (85%)
  matrix products  20.8 us (6%)
  between operations  13.1 us (4%)
  blocking collectives  8.67 us (3%)
  other arithmetic  6.74 us (2%)
    reduce_scatter x1, waiting for transfers between devices, per_device(): lax.psum_scatter(jnp.dot(gathered, proj_matrix, preferred_element_type=jn...  142 us
    all_gather x1, waiting for transfers between devices, per_device(): target_all = lax.all_gather(targets, 'proj', axis=0, tiled=True)  72.2 us
    all_gather x1, waiting for transfers between devices, per_device(): gathered = lax.all_gather(grads, 'grp', axis=0, tiled=True)  55.7 us
    reduce_scatter x1, waiting for transfers between devices, per_device(): lax.psum_scatter(products, 'grp', scatter_dimension=1, tiled=True)  14.8 us
    dot_general x1, matrix products, per_device(): jnp.dot(gathered, proj_matrix, preferred_element_type=jnp.float32)  14.4 us
    psum x1, blocking collectives, per_device(): feature_sq, target_sq = lax.psum((feature_sq, target_sq), 'grp')  8.67 us
  transfers between devices with their start and end apart: 4, of which 4 were waited for; matrix products, arithmetic and copies ran while one was open for 6% of the time, Pallas kernels for 0%

commit v1 on v0

v1 whole, which is shorter than its diff:
```python
import jax
import jax.numpy as jnp
from jax import lax
from jax.experimental import pallas as pl
from jax.experimental.pallas import tpu as pltpu
from jax.sharding import PartitionSpec as P

K = 8192
MESH = pl.DeviceIdType.MESH
NX, NY, NZ, NC = 4, 4, 8, 2
CH, RC, RZ = 4, 64, 8
COLS = 512
LANES = COLS + 256


def kernel(
    g_ref, m_ref, t_ref, out_ref,
    gb, mb, fp, yr, zb, zr, fz, fb, tb, tq, pb, xr, sb, fr,
    loc_sem, gs, gr, ss, sr, ms, mr, ts, tr, tzs, tzr, ys, yrs, zs, zrs, fs, frs, xs, xrs, es, ers,
):
    x = lax.axis_index("grp")
    p = lax.axis_index("proj")
    c = p % NC
    z = (p // NC) % NZ
    y = p // (NC * NZ)
    depth = m_ref.shape[0]
    half = m_ref.shape[1] // NC
    trows = t_ref.shape[0]
    sib = 1 - c

    def dev(dx, dy, dz, dc):
        return ((dy * NZ + dz) * NC + dc, dx)

    here = dev(x, y, z, c)
    right, left = (x + 1) % NX, (x + NX - 1) % NX
    across = (x + 2) % NX

    def remote(src, dst, send, recv, where):
        return pltpu.make_async_remote_copy(
            src_ref=src, dst_ref=dst, send_sem=send, recv_sem=recv,
            device_id=where, device_id_type=MESH,
        )

    def arrived(dst, sem):
        remote(dst, dst, sem, sem, dev(x, y, z, sib)).wait_recv()

    def sent(src, sem):
        remote(src, src, sem, sem, dev(x, y, z, sib)).wait_send()

    own_cols = pl.ds(pl.multiple_of(c * half, half), half)
    sib_cols = pl.ds(pl.multiple_of(sib * half, half), half)
    own_t = tb.at[z, pl.ds(pl.multiple_of(c * trows, trows), trows), :]
    sib_t = tb.at[z, pl.ds(pl.multiple_of(sib * trows, trows), trows), :]

    local = []
    for k in range(CH):
        local.append(pltpu.make_async_copy(
            g_ref.at[pl.ds(k * RC, RC), :], gb.at[0, k, x], loc_sem.at[k]))
    local.append(pltpu.make_async_copy(t_ref.at[:, own_cols], own_t, loc_sem.at[CH]))
    local.append(pltpu.make_async_copy(m_ref.at[:, own_cols], mb.at[0], loc_sem.at[CH + 1]))
    for copy in local:
        copy.start()

    barrier = pltpu.get_barrier_semaphore()
    zo = z // 4
    co = (z // 2) % 2
    for d in range(1, NX):
        pl.semaphore_signal(barrier, inc=1, device_id=dev((x + d) % NX, y, z, c), device_id_type=MESH)
    pl.semaphore_signal(barrier, inc=1, device_id=dev(x, y, z, sib), device_id_type=MESH)
    for d in range(1, NY):
        pl.semaphore_signal(barrier, inc=1, device_id=dev(x, (y + d) % NY, z, c), device_id_type=MESH)
    for d in range(1, NZ):
        pl.semaphore_signal(barrier, inc=1, device_id=dev(x, y, (z + d) % NZ, c), device_id_type=MESH)
    for zp in range(2):
        for cp in range(NC):
            zf = 4 * (z % 2) + 2 * c + zp
            pl.semaphore_signal(barrier, inc=1, device_id=dev(y, x, zf, cp), device_id_type=MESH)
    pl.semaphore_wait(barrier, (NX - 1) + 1 + (NY - 1) + (NZ - 1) + 4)

    def own_sends(k):
        src = g_ref.at[pl.ds(k * RC, RC), :]
        dst = gb.at[0, k, x]
        return [
            remote(src, dst, gs.at[k, 0], gr.at[k, 0], dev(right, y, z, c)),
            remote(src, dst, gs.at[k, 1], gr.at[k, 1], dev(left, y, z, c)),
            remote(src, gb.at[1, k, x], ss.at[k, 0], sr.at[k, 0], dev(x, y, z, sib)),
        ]

    def to_sibling(k, who, slot):
        return remote(gb.at[0, k, who], gb.at[1, k, who], ss.at[k, slot], sr.at[k, slot], dev(x, y, z, sib))

    started = []

    def go(copies):
        for copy in copies:
            copy.start()
            started.append(copy)

    go(own_sends(0))
    go([remote(t_ref.at[:, sib_cols], own_t, ts, tr, dev(x, y, z, sib))])
    go([remote(m_ref.at[:, sib_cols], mb.at[1], ms, mr, dev(x, y, z, sib))])
    go(own_sends(1))

    local[CH].wait()
    arrived(sib_t, tr)
    for d in range(1, NZ):
        go([remote(tb.at[z], tb.at[z], tzs.at[d - 1], tzr.at[d - 1], dev(x, y, (z + d) % NZ, c))])

    def product(k):
        @pl.loop(0, half // 256)
        def _(n):
            cols = pl.ds(pl.multiple_of(n * 256, 256), 256)
            acc = jnp.dot(
                gb[0, k].reshape(NX * RC, depth), mb[0, :, cols], preferred_element_type=jnp.float32)
            acc = acc + jnp.dot(
                gb[1, k].reshape(NX * RC, depth), mb[1, :, cols], preferred_element_type=jnp.float32)
            fp[k, :, :, cols] = acc.reshape(NY, RC, 256)

    def y_stage(k):
        for d in range(1, NY):
            go([remote(fp.at[k, (y + d) % NY], yr.at[k, d - 1], ys.at[k, d - 1], yrs.at[k, d - 1],
                       dev(x, (y + d) % NY, z, c))])

    def z_stage(k):
        for d in range(1, NY):
            arrived(yr.at[k, d - 1], yrs.at[k, d - 1])
        zb[k] = (fp[k, y] + yr[k, 0]) + (yr[k, 1] + yr[k, 2])
        for d in range(1, NZ):
            to = (z + d) % NZ
            go([remote(zb.at[k, pl.ds(pl.multiple_of(to * RZ, RZ), RZ), :], zr.at[k, d - 1],
                       zs.at[k, d - 1], zrs.at[k, d - 1], dev(x, y, to, c))])

    def z_sum(k):
        for d in range(1, NZ):
            arrived(zr.at[k, d - 1], zrs.at[k, d - 1])
        total = zb[k, pl.ds(pl.multiple_of(z * RZ, RZ), RZ), :]
        for d in range(1, NZ):
            total = total + zr[k, d - 1]
        fz[k] = total

    for k in range(CH):
        h = RC // 2
        arrived(gb.at[0, k, left], gr.at[k, 0])
        go([remote(gb.at[0, k, left, pl.ds(0, h), :], gb.at[0, k, left, pl.ds(0, h), :],
                   gs.at[k, 2], gr.at[k, 2], dev(right, y, z, c)),
            to_sibling(k, left, 1)])
        arrived(gb.at[0, k, right], gr.at[k, 1])
        go([remote(gb.at[0, k, right, pl.ds(h, h), :], gb.at[0, k, right, pl.ds(h, h), :],
                   gs.at[k, 3], gr.at[k, 3], dev(left, y, z, c)),
            to_sibling(k, right, 2)])
        if k + 2 < CH:
            go(own_sends(k + 2))
        if k >= 1:
            z_stage(k - 1)
        if k >= 2:
            z_sum(k - 2)
        if k == CH - 1:
            for d in range(1, NZ):
                arrived(tb.at[(z + NZ - d) % NZ], tzr.at[d - 1])
            ones = jnp.ones((8, half), jnp.bfloat16)
            tq[...] = jnp.zeros_like(tq)
            for j in range(COLS // 128):
                sq = jnp.square(tb[pl.ds(2 * j, 2)].reshape(128, half).astype(jnp.float32))
                high = sq.astype(jnp.bfloat16)
                low = (sq - high.astype(jnp.float32)).astype(jnp.bfloat16)
                row = inner_rows(ones, high) + inner_rows(ones, low)
                tq[j:j + 1, :] = row[0:1, :]
        arrived(gb.at[0, k, across, pl.ds(0, h), :], gr.at[k, 2])
        arrived(gb.at[0, k, across, pl.ds(h, h), :], gr.at[k, 3])
        go([to_sibling(k, across, 3)])
        local[k].wait()
        if k == 0:
            local[CH + 1].wait()
            arrived(mb.at[1], mr)
        arrived(gb.at[1, k, x], sr.at[k, 0])
        arrived(gb.at[1, k, left], sr.at[k, 1])
        arrived(gb.at[1, k, right], sr.at[k, 2])
        arrived(gb.at[1, k, across], sr.at[k, 3])
        product(k)
        y_stage(k)

    z_sum(CH - 2)
    z_stage(CH - 1)
    z_sum(CH - 1)
    fb[y] = fz[...].reshape(CH * RZ, half).astype(jnp.bfloat16)

    for d in range(1, NY):
        go([remote(fb.at[y], fb.at[y], fs.at[d - 1], frs.at[d - 1], dev(x, (y + d) % NY, z, c))])
    for d in range(1, NY):
        arrived(fb.at[(y + NY - d) % NY], frs.at[d - 1])
    rows = fb[...].reshape(NY * CH * RZ, half)
    pb[:, :, 0:COLS] = inner_rows(rows, tb[...].reshape(COLS, half)).reshape(NY, CH * RZ, COLS)
    sq = jnp.sum(jnp.square(rows.astype(jnp.float32)), axis=1, keepdims=True)
    pb[:, :, COLS:COLS + 128] = jnp.broadcast_to(sq, (NY * CH * RZ, 128)).reshape(NY, CH * RZ, 128)
    quarter = tq[...]
    for b in range(NY):
        for k in range(CH):
            pb[b, k * RZ:(k + 1) * RZ, COLS + 128:] = quarter

    for d in range(1, NX):
        go([remote(pb.at[(x + d) % NX], xr.at[d - 1], xs.at[d - 1], xrs.at[d - 1],
                   dev((x + d) % NX, y, z, c))])
    for d in range(1, NX):
        arrived(xr.at[d - 1], xrs.at[d - 1])
    sb[...] = ((pb[x] + xr[0]) + (xr[1] + xr[2])).reshape(CH, RZ, LANES)

    for k in range(CH):
        to = 2 * k + zo
        same = (x == y) & (to == z) & (c == co)

        @pl.when(same)
        def _():
            copy = pltpu.make_async_copy(sb.at[k], fr.at[z % 2, c], ers.at[z % 2, c])
            copy.start()

        @pl.when(jnp.logical_not(same))
        def _():
            copy = remote(sb.at[k], fr.at[z % 2, c], es.at[k], ers.at[z % 2, c], dev(y, x, to, co))
            copy.start()
            copy.wait_send()

    for zp in range(2):
        for cp in range(NC):
            arrived(fr.at[zp, cp], ers.at[zp, cp])
        m = fr[zp, 0] + fr[zp, 1]
        tsq = jnp.concatenate([m[j:j + 1, COLS + 128:] for j in range(COLS // 128)], axis=1)
        out_ref[zp * RZ:(zp + 1) * RZ, :] = (
            float(K) ** 0.5
            * m[:, 0:COLS]
            * lax.rsqrt(m[:, COLS:COLS + 1] + 1e-06)
            * lax.rsqrt(tsq + 1e-06)
        )

    for copy in started:
        copy.wait_send()


def inner_rows(left, right):
    return lax.dot_general(
        left, right, (((1,), (1,)), ((), ())), preferred_element_type=jnp.float32
    )


def per_device(grads, proj_matrix, targets):
    depth, dims = proj_matrix.shape
    half = dims // NC
    dma = pltpu.SemaphoreType.DMA
    bf16, f32 = jnp.bfloat16, jnp.float32
    return pl.pallas_call(
        kernel,
        out_shape=jax.ShapeDtypeStruct((2 * RZ, COLS), f32),
        in_specs=[pl.BlockSpec(memory_space=pltpu.HBM)] * 3,
        out_specs=pl.BlockSpec(memory_space=pltpu.VMEM),
        scratch_shapes=[
            pltpu.VMEM((NC, CH, NX, RC, depth), bf16),
            pltpu.VMEM((NC, depth, half), bf16),
            pltpu.VMEM((CH, NY, RC, half), f32),
            pltpu.VMEM((CH, NY - 1, RC, half), f32),
            pltpu.VMEM((CH, RC, half), f32),
            pltpu.VMEM((CH, NZ - 1, RZ, half), f32),
            pltpu.VMEM((CH, RZ, half), f32),
            pltpu.VMEM((NY, CH * RZ, half), bf16),
            pltpu.VMEM((NZ, NC * targets.shape[0], half), bf16),
            pltpu.VMEM((8, 128), f32),
            pltpu.VMEM((NY, CH * RZ, LANES), f32),
            pltpu.VMEM((NX - 1, CH * RZ, LANES), f32),
            pltpu.VMEM((CH, RZ, LANES), f32),
            pltpu.VMEM((2, NC, RZ, LANES), f32),
            dma((CH + 2,)),
            dma((CH, 4)), dma((CH, 4)), dma((CH, 4)), dma((CH, 4)),
            dma, dma, dma, dma,
            dma((NZ - 1,)), dma((NZ - 1,)),
            dma((CH, NY - 1)), dma((CH, NY - 1)),
            dma((CH, NZ - 1)), dma((CH, NZ - 1)),
            dma((NY - 1,)), dma((NY - 1,)),
            dma((NX - 1,)), dma((NX - 1,)),
            dma((CH,)), dma((2, NC)),
        ],
        compiler_params=pltpu.CompilerParams(
            collective_id=0, has_side_effects=True, vmem_limit_bytes=56 * 1024 * 1024
        ),
    )(grads, proj_matrix, targets)


def solution(mesh):
    placed = (P("grp", "proj"), P("proj", "grp"), P("proj", "grp"))
    return jax.shard_map(
        per_device, mesh=mesh, in_specs=placed, out_specs=P("proj", "grp"), check_vma=False
    )
```

time: 338 us -> 131 us (0.39)
  the two profiles are of different devices: /device:TPU:1 before, /device:TPU:240 now
where the time goes in v1:
time: 131 us
  Pallas kernels  129 us (98%)
  local copies, waits for them, and re-layouts  1.38 us (1%)
    pallas_call x1, Pallas kernels, per_device(): pl.pallas_call(kernel, out_shape=jax.ShapeDtypeStruct((2 * RZ, COLS), f32...  129 us

profile of v1, /device:TPU:240, one launch (start us, length us, event | category | flops | bytes accessed | tf_op | source)
XLA Modules:
  0.0 130.7 jit_solution(7425967937002604596)
XLA Ops:
  0.0 129.3 %shard_map.37 = f32[16,512]{1,0:T(8,128)} custom-call(bf16[256,2048]{1,0:T(8,128)(2,1)} %g_ref.1, bf16[2048,2048]{1,0:T(8,128)(2,1)} %m_ref.1, bf16[32,2048]{1,0:T(8,128)(2,1)} %t_ref.1), custom_call_target="tpu_custom_call" | custom-call | tf_op jit(solution)/shard_map/pallas_call | solution.py:249
  129.3 1.4 %copy.5 = f32[16,512]{1,0:T(8,128)} copy(f32[16,512]{1,0:T(8,128)} %shard_map.37) | data formatting | bytes 65536

commit v2 on v1

v2 whole, which is shorter than its diff:
```python
import jax
import jax.numpy as jnp
from jax import lax
from jax.experimental import pallas as pl
from jax.experimental.pallas import tpu as pltpu
from jax.sharding import PartitionSpec as P

K = 8192
MESH = pl.DeviceIdType.MESH
NX, NY, NZ, NC = 4, 4, 8, 2
CH, RC, RZ, HP = 4, 64, 8, 2
COLS = 512
LANES = COLS + 256


def inner_rows(left, right):
    return lax.dot_general(
        left, right, (((1,), (1,)), ((), ())), preferred_element_type=jnp.float32
    )


def kernel(
    g_ref, m_ref, t_ref, out_ref,
    gb, mb, fo, fp, yr, zb, zr, fb, tb, tq, pb, fr,
    gl, loc, gs, gr, ss, sr, ms, mr, ts, tr, tzs, tzr, ys, yrs, zs, zrs, fs, frs, es, ers,
):
    x = lax.axis_index("grp")
    p = lax.axis_index("proj")
    c = p % NC
    z = (p // NC) % NZ
    y = p // (NC * NZ)
    depth = m_ref.shape[0]
    half = m_ref.shape[1] // NC
    part = half // HP
    trows = t_ref.shape[0]
    sib = 1 - c

    def dev(dx, dy, dz, dc):
        return ((dy * NZ + dz) * NC + dc, dx)

    right, left = (x + 1) % NX, (x + NX - 1) % NX
    across = (x + 2) % NX

    def remote(src, dst, send, recv, where):
        return pltpu.make_async_remote_copy(
            src_ref=src, dst_ref=dst, send_sem=send, recv_sem=recv,
            device_id=where, device_id_type=MESH,
        )

    def arrived(dst, sem):
        remote(dst, dst, sem, sem, dev(x, y, z, sib)).wait_recv()

    own_cols = pl.ds(pl.multiple_of(c * half, half), half)
    sib_cols = pl.ds(pl.multiple_of(sib * half, half), half)
    own_t = tb.at[z, pl.ds(pl.multiple_of(c * trows, trows), trows), :]
    sib_t = tb.at[z, pl.ds(pl.multiple_of(sib * trows, trows), trows), :]

    g_local = []
    for k in range(CH):
        g_local.append([
            pltpu.make_async_copy(
                g_ref.at[pl.ds(w * CH * RZ + k * RZ, RZ), :],
                gb.at[0, k, x, pl.ds(w * RZ, RZ), :], gl.at[k, w])
            for w in range(NZ)
        ])
    t_local = pltpu.make_async_copy(t_ref.at[:, own_cols], own_t, loc.at[0])
    m_local = pltpu.make_async_copy(m_ref.at[:, own_cols], mb.at[0], loc.at[1])
    for k in range(CH):
        for copy in g_local[k]:
            copy.start()
        if k == 0:
            t_local.start()
    m_local.start()

    barrier = pltpu.get_barrier_semaphore()

    def greet(where):
        pl.semaphore_signal(barrier, inc=1, device_id=where, device_id_type=MESH)

    for xs in range(NX):
        for cs in range(NC):
            greet(dev(xs, x, z, cs))
    for d in range(1, NZ):
        greet(dev(x, y, (z + d) % NZ, c))
    for d in range(1, NY):
        greet(dev(x, (y + d) % NY, z, c))
    greet(dev(right, y, z, c))
    greet(dev(left, y, z, c))
    greet(dev(x, y, z, sib))
    pl.semaphore_wait(barrier, NX * NC + (NZ - 1) + (NY - 1) + 3)

    started = []

    def go(copies):
        for copy in copies:
            copy.start()
            started.append(copy)

    def to_sibling(k, who, slot):
        return remote(gb.at[0, k, who], gb.at[1, k, who], ss.at[k, slot], sr.at[k, slot], dev(x, y, z, sib))

    def own_sends(k):
        for copy in g_local[k]:
            copy.wait()
        block = gb.at[0, k, x]
        go([
            remote(block, block, gs.at[k, 0], gr.at[k, 0], dev(right, y, z, c)),
            remote(block, block, gs.at[k, 1], gr.at[k, 1], dev(left, y, z, c)),
            to_sibling(k, x, 0),
        ])

    own_sends(0)
    go([remote(t_ref.at[:, sib_cols], own_t, ts, tr, dev(x, y, z, sib))])
    go([remote(m_ref.at[:, sib_cols], mb.at[1], ms, mr, dev(x, y, z, sib))])
    own_sends(1)

    t_local.wait()
    arrived(sib_t, tr)
    for d in range(1, NZ):
        go([remote(tb.at[z], tb.at[z], tzs.at[d - 1], tzr.at[d - 1], dev(x, y, (z + d) % NZ, c))])

    def product(k, h):
        @pl.loop(0, part // 256)
        def _(n):
            first = pl.multiple_of(n * 256, 256)
            cols = pl.ds(h * part + first, 256)
            acc = jnp.dot(
                gb[0, k].reshape(NX * RC, depth), mb[0, :, cols], preferred_element_type=jnp.float32)
            acc = acc + jnp.dot(
                gb[1, k].reshape(NX * RC, depth), mb[1, :, cols], preferred_element_type=jnp.float32)
            acc = acc.reshape(NY, RC, 256)
            fo[k, h, :, :, pl.ds(first, 256)] = acc
            fp[k, h, :, :, pl.ds(first, 256)] = acc.astype(jnp.bfloat16)

    def y_send(k, h):
        for d in range(1, NY):
            to = (y + d) % NY
            go([remote(fp.at[k, h, to], yr.at[k, h, d - 1], ys.at[k, h, d - 1], yrs.at[k, h, d - 1],
                       dev(x, to, z, c))])

    def z_stage(k, h):
        for d in range(1, NY):
            arrived(yr.at[k, h, d - 1], yrs.at[k, h, d - 1])
        total = fo[k, h, y]
        for d in range(1, NY):
            total = total + yr[k, h, d - 1].astype(jnp.float32)
        zb[k, h] = total
        for d in range(1, NZ):
            to = (z + d) % NZ
            go([remote(zb.at[k, h, pl.ds(pl.multiple_of(to * RZ, RZ), RZ), :], zr.at[k, h, d - 1],
                       zs.at[k, h, d - 1], zrs.at[k, h, d - 1], dev(x, y, to, c))])

    def z_sum(k):
        for h in range(HP):
            for d in range(1, NZ):
                arrived(zr.at[k, h, d - 1], zrs.at[k, h, d - 1])
            total = zb[k, h, pl.ds(pl.multiple_of(z * RZ, RZ), RZ), :]
            for d in range(1, NZ):
                total = total + zr[k, h, d - 1]
            fb[k, y, :, h * part:(h + 1) * part] = total
        for d in range(1, NY):
            to = (y + d) % NY
            go([remote(fb.at[k, y], fb.at[k, y], fs.at[k, d - 1], frs.at[k, d - 1], dev(x, to, z, c))])

    def target_squares():
        for d in range(1, NZ):
            arrived(tb.at[(z + NZ - d) % NZ], tzr.at[d - 1])
        ones = jnp.ones((8, half), jnp.bfloat16)
        tq[...] = jnp.zeros_like(tq)
        for j in range(COLS // 128):
            sq = jnp.square(tb[pl.ds(2 * j, 2)].reshape(128, half).astype(jnp.float32))
            high = sq.astype(jnp.bfloat16)
            low = (sq - high.astype(jnp.float32)).astype(jnp.bfloat16)
            row = inner_rows(ones, high) + inner_rows(ones, low)
            tq[j:j + 1, :] = row[0:1, :]

    def owner_copy(k, d):
        to = (y + d) % NY
        cc, hh = k // 2, k % 2
        return remote(pb.at[k, to], fr.at[hh, x, c], es.at[k, d], ers.at[hh, x, c], dev(y, to, z, cc))

    def scores(k):
        for d in range(1, NY):
            arrived(fb.at[k, (y + NY - d) % NY], frs.at[k, d - 1])
        rows = fb[k].reshape(NY * RZ, half)
        high = rows.astype(jnp.bfloat16)
        low = (rows - high.astype(jnp.float32)).astype(jnp.bfloat16)
        both = inner_rows(jnp.concatenate([high, low], axis=0), tb[...].reshape(COLS, half))
        pb[k, :, :, 0:COLS] = (both[:NY * RZ] + both[NY * RZ:]).reshape(NY, RZ, COLS)
        sq = jnp.sum(jnp.square(rows), axis=1, keepdims=True)
        pb[k, :, :, COLS:COLS + 128] = jnp.broadcast_to(sq, (NY * RZ, 128)).reshape(NY, RZ, 128)
        pb[k, :, :, COLS + 128:] = jnp.broadcast_to(tq[...][None], (NY, RZ, 128))
        same = (x == y) & (c == k // 2)

        @pl.when(same)
        def _():
            pltpu.make_async_copy(pb.at[k, y], fr.at[k % 2, x, c], ers.at[k % 2, x, c]).start()

        @pl.when(jnp.logical_not(same))
        def _():
            owner_copy(k, 0).start()

        for d in range(1, NY):
            go([owner_copy(k, d)])

    h = RC // 2
    for k in range(CH):
        arrived(gb.at[0, k, left], gr.at[k, 0])
        go([remote(gb.at[0, k, left, pl.ds(0, h), :], gb.at[0, k, left, pl.ds(0, h), :],
                   gs.at[k, 2], gr.at[k, 2], dev(right, y, z, c)),
            to_sibling(k, left, 1)])
        arrived(gb.at[0, k, right], gr.at[k, 1])
        go([remote(gb.at[0, k, right, pl.ds(h, h), :], gb.at[0, k, right, pl.ds(h, h), :],
                   gs.at[k, 3], gr.at[k, 3], dev(left, y, z, c)),
            to_sibling(k, right, 2)])
        if k + 2 < CH:
            own_sends(k + 2)
        if k >= 1:
            z_stage(k - 1, 0)
            z_stage(k - 1, 1)
        if k >= 2:
            z_sum(k - 2)
        if k == CH - 1:
            target_squares()
            scores(k - 3)
        arrived(gb.at[0, k, across, pl.ds(0, h), :], gr.at[k, 2])
        arrived(gb.at[0, k, across, pl.ds(h, h), :], gr.at[k, 3])
        go([to_sibling(k, across, 3)])
        if k == 0:
            m_local.wait()
            arrived(mb.at[1], mr)
        arrived(gb.at[1, k, x], sr.at[k, 0])
        arrived(gb.at[1, k, left], sr.at[k, 1])
        arrived(gb.at[1, k, right], sr.at[k, 2])
        arrived(gb.at[1, k, across], sr.at[k, 3])
        for q in range(HP):
            product(k, q)
            y_send(k, q)

    z_sum(CH - 2)
    scores(CH - 3)
    z_stage(CH - 1, 0)
    z_stage(CH - 1, 1)
    scores(CH - 2)
    z_sum(CH - 1)
    scores(CH - 1)

    for hh in range(2):
        m = None
        for xs in range(NX):
            for cs in range(NC):
                arrived(fr.at[hh, xs, cs], ers.at[hh, xs, cs])
        m = fr[hh, 0, 0]
        for s in range(1, NX * NC):
            m = m + fr[hh, s // NC, s % NC]
        tsq = jnp.concatenate([m[j:j + 1, COLS + 128:] for j in range(COLS // 128)], axis=1)
        out_ref[hh * RZ:(hh + 1) * RZ, :] = (
            float(K) ** 0.5
            * m[:, 0:COLS]
            * lax.rsqrt(m[:, COLS:COLS + 1] + 1e-06)
            * lax.rsqrt(tsq + 1e-06)
        )

    for copy in started:
        copy.wait_send()
    for k in range(CH):
        @pl.when(jnp.logical_not((x == y) & (c == k // 2)))
        def _():
            owner_copy(k, 0).wait_send()


def per_device(grads, proj_matrix, targets):
    depth, dims = proj_matrix.shape
    half = dims // NC
    part = half // HP
    dma = pltpu.SemaphoreType.DMA
    bf16, f32 = jnp.bfloat16, jnp.float32
    return pl.pallas_call(
        kernel,
        out_shape=jax.ShapeDtypeStruct((2 * RZ, COLS), f32),
        in_specs=[pl.BlockSpec(memory_space=pltpu.HBM)] * 3,
        out_specs=pl.BlockSpec(memory_space=pltpu.VMEM),
        scratch_shapes=[
            pltpu.VMEM((NC, CH, NX, RC, depth), bf16),
            pltpu.VMEM((NC, depth, half), bf16),
            pltpu.VMEM((CH, HP, NY, RC, part), f32),
            pltpu.VMEM((CH, HP, NY, RC, part), bf16),
            pltpu.VMEM((CH, HP, NY - 1, RC, part), bf16),
            pltpu.VMEM((CH, HP, RC, part), f32),
            pltpu.VMEM((CH, HP, NZ - 1, RZ, part), f32),
            pltpu.VMEM((CH, NY, RZ, half), f32),
            pltpu.VMEM((NZ, NC * targets.shape[0], half), bf16),
            pltpu.VMEM((8, 128), f32),
            pltpu.VMEM((CH, NY, RZ, LANES), f32),
            pltpu.VMEM((2, NX, NC, RZ, LANES), f32),
            dma((CH, NZ)), dma((2,)),
            dma((CH, 4)), dma((CH, 4)), dma((CH, 4)), dma((CH, 4)),
            dma, dma, dma, dma,
            dma((NZ - 1,)), dma((NZ - 1,)),
            dma((CH, HP, NY - 1)), dma((CH, HP, NY - 1)),
            dma((CH, HP, NZ - 1)), dma((CH, HP, NZ - 1)),
            dma((CH, NY - 1)), dma((CH, NY - 1)),
            dma((CH, NY)), dma((2, NX, NC)),
        ],
        compiler_params=pltpu.CompilerParams(
            collective_id=0, has_side_effects=True, vmem_limit_bytes=56 * 1024 * 1024
        ),
    )(grads, proj_matrix, targets)


def solution(mesh):
    placed = (P("grp", "proj"), P("proj", "grp"), P("proj", "grp"))
    return jax.shard_map(
        per_device, mesh=mesh, in_specs=placed, out_specs=P("proj", "grp"), check_vma=False
    )
```

time: 131 us -> 95 us (0.73)
  the two profiles are of different devices: /device:TPU:240 before, /device:TPU:1 now
where the time goes in v2:
time: 95 us; the launch traced here: 94.7 us
  Pallas kernels  93.3 us (98%)
  local copies, waits for them, and re-layouts  1.38 us (1%)
    pallas_call x1, Pallas kernels, per_device(): pl.pallas_call(kernel, out_shape=jax.ShapeDtypeStruct((2 * RZ, COLS), f32...  93.3 us

profile of v2, /device:TPU:1, one launch (start us, length us, event | category | flops | bytes accessed | tf_op | source)
XLA Modules:
  0.0 94.7 jit_solution(738154986416139306)
XLA Ops:
  0.0 93.3 %shard_map.37 = f32[16,512]{1,0:T(8,128)} custom-call(bf16[256,2048]{1,0:T(8,128)(2,1)} %g_ref.1, bf16[2048,2048]{1,0:T(8,128)(2,1)} %m_ref.1, bf16[32,2048]{1,0:T(8,128)(2,1)} %t_ref.1), custom_call_target="tpu_custom_call" | custom-call | tf_op jit(solution)/shard_map/pallas_call | solution.py:278
  93.4 1.4 %copy.5 = f32[16,512]{1,0:T(8,128)} copy(f32[16,512]{1,0:T(8,128)} %shard_map.37) | data formatting | bytes 65536

commit v3 on v2

v3 whole, which is shorter than its diff:
```python
import jax
import jax.numpy as jnp
from jax import lax
from jax.experimental import pallas as pl
from jax.experimental.pallas import tpu as pltpu
from jax.sharding import PartitionSpec as P

K = 8192
MESH = pl.DeviceIdType.MESH
NX, NY, NZ, NC = 4, 4, 8, 2
CH, RC, RZ, HP = 4, 64, 8, 2
COLS, TILE = 512, 128


def inner_rows(left, right):
    return lax.dot_general(
        left, right, (((1,), (1,)), ((), ())), preferred_element_type=jnp.float32
    )


def kernel(
    g_ref, m_ref, t_ref, out_ref,
    gb, mb, fo, fp, yr, zb, zq, zr, zt, fb, tb, order, pb, fr,
    gl, loc, gs, gr, ss, sr, ms, mr, ts, tr, tzs, tzr, ys, yrs, zs, zrs, fs, frs, es, ers,
):
    x = lax.axis_index("grp")
    p = lax.axis_index("proj")
    c = p % NC
    z = (p // NC) % NZ
    y = p // (NC * NZ)
    depth = m_ref.shape[0]
    half = m_ref.shape[1] // NC
    part = half // HP
    sib = 1 - c

    def dev(dx, dy, dz, dc):
        return ((dy * NZ + dz) * NC + dc, dx)

    right, left = (x + 1) % NX, (x + NX - 1) % NX
    across = (x + 2) % NX

    def remote(src, dst, send, recv, where):
        return pltpu.make_async_remote_copy(
            src_ref=src, dst_ref=dst, send_sem=send, recv_sem=recv,
            device_id=where, device_id_type=MESH,
        )

    def arrived(dst, sem):
        remote(dst, dst, sem, sem, dev(x, y, z, sib)).wait_recv()

    own_cols = pl.ds(pl.multiple_of(c * half, half), half)
    sib_cols = pl.ds(pl.multiple_of(sib * half, half), half)
    g_local = []
    for k in range(CH):
        g_local.append([
            pltpu.make_async_copy(
                g_ref.at[pl.ds(w * CH * RZ + k * RZ, RZ), :],
                gb.at[0, k, x, pl.ds(w * RZ, RZ), :], gl.at[k, w])
            for w in range(NZ)
        ])
    m_local = pltpu.make_async_copy(m_ref.at[:, own_cols], mb.at[0], loc.at[1])
    for k in range(CH):
        for copy in g_local[k]:
            copy.start()
    m_local.start()

    barrier = pltpu.get_barrier_semaphore()

    def greet(where):
        pl.semaphore_signal(barrier, inc=1, device_id=where, device_id_type=MESH)

    for dx in range(NX):
        for dy in range(NY):
            for cs in range(NC):
                greet(dev((x + dx) % NX, (y + dy) % NY, z, cs))
    for d in range(1, NZ):
        greet(dev(x, y, (z + d) % NZ, c))
    pl.semaphore_wait(barrier, NX * NY * NC + NZ - 1)

    started = []

    def go(copies):
        for copy in copies:
            copy.start()
            started.append(copy)

    def to_sibling(k, who, slot):
        return remote(gb.at[0, k, who], gb.at[1, k, who], ss.at[k, slot], sr.at[k, slot], dev(x, y, z, sib))

    def rows_of(k, who, which):
        return gb.at[0, k, who, pl.ds(which * (RC // 2), RC // 2), :]

    def own_sends(k):
        for copy in g_local[k]:
            copy.wait()
        first, last = rows_of(k, x, 0), rows_of(k, x, 1)
        go([
            remote(first, first, gs.at[k, 0], gr.at[k, 0], dev(right, y, z, c)),
            remote(last, last, gs.at[k, 2], gr.at[k, 2], dev(left, y, z, c)),
            remote(last, last, gs.at[k, 1], gr.at[k, 1], dev(right, y, z, c)),
            remote(first, first, gs.at[k, 3], gr.at[k, 3], dev(left, y, z, c)),
            to_sibling(k, x, 0),
        ])

    own_sends(0)
    trows = t_ref.shape[0] // HP

    def deal(j, cc):
        source = t_ref.at[pl.ds(j * trows, trows), pl.ds(cc * half, half)]
        to = HP * c + j
        same = (to == y) & (cc == c)
        return same, remote(source, tb.at[y, z], ts.at[j, cc], tr, dev(x, to, z, cc)), source

    for j in range(HP):
        for cc in range(NC):
            same, copy, source = deal(j, cc)

            @pl.when(same)
            def _():
                pltpu.make_async_copy(source, tb.at[y, z], tr).start()

            @pl.when(jnp.logical_not(same))
            def _():
                copy.start()

    go([remote(m_ref.at[:, sib_cols], mb.at[1], ms, mr, dev(x, y, z, sib))])
    own_sends(1)

    arrived(tb.at[:, z], tr)
    for d in range(1, NZ):
        go([remote(tb.at[:, z], tb.at[:, z], tzs.at[d - 1], tzr.at[d - 1], dev(x, y, (z + d) % NZ, c))])

    def own_product(k):
        @pl.loop(0, half // 256)
        def _(n):
            cols = pl.ds(pl.multiple_of(n * 256, 256), 256)
            acc = jnp.dot(
                gb[0, k].reshape(NX * RC, depth), mb[0, :, cols], preferred_element_type=jnp.float32)
            fo[k, n // (part // 256), :, :, pl.ds(pl.multiple_of(n % (part // 256) * 256, 256), 256)] = (
                acc.reshape(NY, RC, 256))

    def sibling_product(k, h):
        @pl.loop(0, part // 256)
        def _(n):
            first = pl.multiple_of(n * 256, 256)
            cols = pl.ds(h * part + first, 256)
            acc = jnp.dot(
                gb[1, k].reshape(NX * RC, depth), mb[1, :, cols], preferred_element_type=jnp.float32)
            acc = fo[k, h, :, :, pl.ds(first, 256)] + acc.reshape(NY, RC, 256)
            fo[k, h, :, :, pl.ds(first, 256)] = acc
            fp[k, h, :, :, pl.ds(first, 256)] = acc.astype(jnp.bfloat16)

    def y_send(k, h):
        for d in range(1, NY):
            to = (y + d) % NY
            go([remote(fp.at[k, h, to], yr.at[k, h, d - 1], ys.at[k, h, d - 1], yrs.at[k, h, d - 1],
                       dev(x, to, z, c))])

    def z_slot(k, h, d):
        return zt.at[h, d - 1] if k == CH - 1 else zr.at[k, h, d - 1]

    def z_stage(k, h):
        for d in range(1, NY):
            arrived(yr.at[k, h, d - 1], yrs.at[k, h, d - 1])
        total = fo[k, h, y]
        for d in range(1, NY):
            total = total + yr[k, h, d - 1].astype(jnp.float32)
        zb[k, h] = total
        source = zb.at[k, h]
        if k == CH - 1:
            zq[h] = total.astype(jnp.bfloat16)
            source = zq.at[h]
        for d in range(1, NZ):
            to = (z + d) % NZ
            piece = pl.ds(pl.multiple_of(to * RZ, RZ), RZ)
            go([remote(source.at[piece, :], z_slot(k, h, d),
                       zs.at[k, h, d - 1], zrs.at[k, h, d - 1], dev(x, y, to, c))])

    def z_sum(k):
        for h in range(HP):
            for d in range(1, NZ):
                arrived(z_slot(k, h, d), zrs.at[k, h, d - 1])
            total = zb[k, h, pl.ds(pl.multiple_of(z * RZ, RZ), RZ), :]
            for d in range(1, NZ):
                total = total + z_slot(k, h, d)[...].astype(jnp.float32)
            fb[k, y, :, h * part:(h + 1) * part] = total
        for d in range(1, NY):
            to = (y + d) % NY
            go([remote(fb.at[k, y], fb.at[k, y], fs.at[k, d - 1], frs.at[k, d - 1], dev(x, to, z, c))])

    def target_squares():
        for d in range(1, NZ):
            arrived(tb.at[:, (z + NZ - d) % NZ], tzr.at[d - 1])
        ones = jnp.ones((8, half), jnp.bfloat16)
        for b in range(NX):
            sq = jnp.square(tb[b].reshape(TILE, half).astype(jnp.float32))
            high = sq.astype(jnp.bfloat16)
            low = (sq - high.astype(jnp.float32)).astype(jnp.bfloat16)
            row = inner_rows(ones, high) + inner_rows(ones, low)
            for k in range(CH):
                pb[k, :, b, RZ:, :] = jnp.broadcast_to(row[None], (NY, 8, TILE))
        step = COLS // (NY * NZ)
        rows = lax.broadcasted_iota(jnp.int32, (COLS, COLS), 0)
        cols = lax.broadcasted_iota(jnp.int32, (COLS, COLS), 1)
        moved = (rows % TILE) // step * (NY * step) + rows // TILE * step + rows % step
        order[...] = jnp.where(moved == cols, 1.0, 0.0).astype(jnp.bfloat16)

    def owner_copy(k, dx, dy):
        tx, ty = (x + dx) % NX, (y + dy) % NY
        return remote(pb.at[k, ty, tx], fr.at[k % 2, y, x, c], es.at[k], ers.at[k % 2], dev(tx, ty, z, k // 2))

    def scores(k):
        for d in range(1, NY):
            arrived(fb.at[k, (y + NY - d) % NY], frs.at[k, d - 1])
        rows = fb[k].reshape(NY * RZ, half)
        high = rows.astype(jnp.bfloat16)
        low = (rows - high.astype(jnp.float32)).astype(jnp.bfloat16)
        both = inner_rows(jnp.concatenate([high, low], axis=0), tb[...].reshape(COLS, half))
        both = both[:NY * RZ] + both[NY * RZ:]
        sq = jnp.square(rows)
        high = sq.astype(jnp.bfloat16)
        low = (sq - high.astype(jnp.float32)).astype(jnp.bfloat16)
        ones = jnp.ones((8, half), jnp.bfloat16)
        norms = inner_rows(ones, high) + inner_rows(ones, low)
        for b in range(NX):
            pb[k, :, b, 0:RZ, :] = both[:, b * TILE:(b + 1) * TILE].reshape(NY, RZ, TILE)
            for a in range(NY):
                pb[k, a, b, RZ + 1:RZ + 2, 0:NY * RZ] = norms[0:1, :]
        same = c == k // 2

        @pl.when(same)
        def _():
            pltpu.make_async_copy(pb.at[k, y, x], fr.at[k % 2, y, x, c], ers.at[k % 2]).start()

        @pl.when(jnp.logical_not(same))
        def _():
            owner_copy(k, 0, 0).start()

        for dx in range(NX):
            for dy in range(NY):
                if dx or dy:
                    owner_copy(k, dx, dy).start()

    def forward(k):
        arrived(rows_of(k, left, 0), gr.at[k, 0])
        go([remote(rows_of(k, left, 0), rows_of(k, left, 0), gs.at[k, 4], gr.at[k, 4], dev(right, y, z, c))])
        arrived(rows_of(k, right, 1), gr.at[k, 2])
        go([remote(rows_of(k, right, 1), rows_of(k, right, 1), gs.at[k, 5], gr.at[k, 5], dev(left, y, z, c))])

    def dots(k):
        arrived(rows_of(k, left, 1), gr.at[k, 1])
        go([to_sibling(k, left, 1)])
        arrived(rows_of(k, right, 0), gr.at[k, 3])
        go([to_sibling(k, right, 2)])
        arrived(rows_of(k, across, 0), gr.at[k, 4])
        arrived(rows_of(k, across, 1), gr.at[k, 5])
        go([to_sibling(k, across, 3)])
        if k == 0:
            m_local.wait()
        own_product(k)
        if k == 0:
            arrived(mb.at[1], mr)
        arrived(gb.at[1, k, x], sr.at[k, 0])
        arrived(gb.at[1, k, left], sr.at[k, 1])
        arrived(gb.at[1, k, right], sr.at[k, 2])
        arrived(gb.at[1, k, across], sr.at[k, 3])
        for q in range(HP):
            sibling_product(k, q)
            y_send(k, q)

    def z_stages(k):
        for q in range(HP):
            z_stage(k, q)

    forward(0)
    forward(1)
    own_sends(2)
    dots(0)
    dots(1)
    forward(2)
    own_sends(3)
    target_squares()
    z_stages(0)
    forward(3)
    dots(2)
    z_stages(1)
    dots(3)
    z_stages(2)
    z_sum(0)
    z_sum(1)
    z_stages(3)
    scores(0)
    scores(1)
    z_sum(2)
    z_sum(3)
    scores(2)
    scores(3)

    for hh in range(2):
        arrived(fr.at[hh], ers.at[hh])
        blocks = []
        for b in range(NY):
            m = fr[hh, b, 0, 0]
            for q in range(1, NX * NC):
                m = m + fr[hh, b, q // NC, q % NC]
            blocks.append(m)
        m = jnp.concatenate(blocks, axis=1)
        parts = []
        for _ in range(3):
            parts.append(m.astype(jnp.bfloat16))
            m = m - parts[-1].astype(jnp.float32)
        m = jnp.dot(jnp.concatenate(parts, axis=0), order[...], preferred_element_type=jnp.float32)
        m = (m[0:2 * RZ] + m[2 * RZ:4 * RZ]) + m[4 * RZ:]
        row = lax.broadcasted_iota(jnp.int32, (RZ, TILE), 0)
        lane = lax.broadcasted_iota(jnp.int32, (RZ, TILE), 1)
        norms = jnp.broadcast_to(blocks[0][RZ + 1:RZ + 2, :], (RZ, TILE))
        fsq = jnp.sum(jnp.where(lane == y * RZ + row, norms, 0.0), axis=1, keepdims=True)
        out_ref[hh * RZ:(hh + 1) * RZ, :] = (
            float(K) ** 0.5
            * m[0:RZ]
            * lax.rsqrt(fsq + 1e-06)
            * lax.rsqrt(m[RZ:RZ + 1] + 1e-06)
        )

    for copy in started:
        copy.wait_send()
    for k in range(CH):
        def leave(block):
            remote(block, block, es.at[k], es.at[k], dev(x, y, z, sib)).wait_send()

        leave(pb.at[k, 0:NY - 1])
        leave(pb.at[k, 0, 0:NX - 1])

        @pl.when(c != k // 2)
        def _():
            leave(pb.at[k, 0, 0])
    for j in range(HP):
        for cc in range(NC):
            same, copy, source = deal(j, cc)

            @pl.when(jnp.logical_not(same))
            def _():
                copy.wait_send()


def per_device(grads, proj_matrix, targets):
    depth, dims = proj_matrix.shape
    half = dims // NC
    part = half // HP
    dma = pltpu.SemaphoreType.DMA
    bf16, f32 = jnp.bfloat16, jnp.float32
    return pl.pallas_call(
        kernel,
        out_shape=jax.ShapeDtypeStruct((2 * RZ, COLS), f32),
        in_specs=[pl.BlockSpec(memory_space=pltpu.HBM)] * 3,
        out_specs=pl.BlockSpec(memory_space=pltpu.VMEM),
        scratch_shapes=[
            pltpu.VMEM((NC, CH, NX, RC, depth), bf16),
            pltpu.VMEM((NC, depth, half), bf16),
            pltpu.VMEM((CH, HP, NY, RC, part), f32),
            pltpu.VMEM((CH, HP, NY, RC, part), bf16),
            pltpu.VMEM((CH, HP, NY - 1, RC, part), bf16),
            pltpu.VMEM((CH, HP, RC, part), f32),
            pltpu.VMEM((HP, RC, part), bf16),
            pltpu.VMEM((CH - 1, HP, NZ - 1, RZ, part), f32),
            pltpu.VMEM((HP, NZ - 1, RZ, part), bf16),
            pltpu.VMEM((CH, NY, RZ, half), f32),
            pltpu.VMEM((NY, NZ, targets.shape[0] // HP, half), bf16),
            pltpu.VMEM((COLS, COLS), bf16),
            pltpu.VMEM((CH, NY, NX, 2 * RZ, TILE), f32),
            pltpu.VMEM((2, NY, NX, NC, 2 * RZ, TILE), f32),
            dma((CH, NZ)), dma((2,)),
            dma((CH, 6)), dma((CH, 6)), dma((CH, 4)), dma((CH, 4)),
            dma, dma, dma((HP, NC)), dma,
            dma((NZ - 1,)), dma((NZ - 1,)),
            dma((CH, HP, NY - 1)), dma((CH, HP, NY - 1)),
            dma((CH, HP, NZ - 1)), dma((CH, HP, NZ - 1)),
            dma((CH, NY - 1)), dma((CH, NY - 1)),
            dma((CH,)), dma((2,)),
        ],
        compiler_params=pltpu.CompilerParams(
            collective_id=0, has_side_effects=True, vmem_limit_bytes=56 * 1024 * 1024
        ),
    )(grads, proj_matrix, targets)


def solution(mesh):
    placed = (P("grp", "proj"), P("proj", "grp"), P("proj", "grp"))
    return jax.shard_map(
        per_device, mesh=mesh, in_specs=placed, out_specs=P("proj", "grp"), check_vma=False
    )
```

time: 95 us -> 83 us (0.87)
  Pallas kernels: 93.3 us -> 81.5 us
    pallas_call x1, Pallas kernels: 93.3 us -> 81.5 us  [per_device(): pl.pallas_call(kernel, out_shape=jax.ShapeDtypeStruct((2 * RZ, COLS), f32...]
where the time goes in v3:
time: 83 us; the launch traced here: 82.9 us
  Pallas kernels  81.5 us (98%)
  local copies, waits for them, and re-layouts  1.38 us (2%)
    pallas_call x1, Pallas kernels, per_device(): pl.pallas_call(kernel, out_shape=jax.ShapeDtypeStruct((2 * RZ, COLS), f32...  81.5 us

profile of v3, /device:TPU:1, one launch (start us, length us, event | category | flops | bytes accessed | tf_op | source)
XLA Modules:
  0.0 82.9 jit_solution(8618000215359246389)
XLA Ops:
  0.0 81.5 %shard_map.37 = f32[16,512]{1,0:T(8,128)} custom-call(bf16[256,2048]{1,0:T(8,128)(2,1)} %g_ref.1, bf16[2048,2048]{1,0:T(8,128)(2,1)} %m_ref.1, bf16[32,2048]{1,0:T(8,128)(2,1)} %t_ref.1), custom_call_target="tpu_custom_call" | custom-call | tf_op jit(solution)/shard_map/pallas_call | solution.py:352
  81.5 1.4 %copy.5 = f32[16,512]{1,0:T(8,128)} copy(f32[16,512]{1,0:T(8,128)} %shard_map.37) | data formatting | bytes 65536

commit v4 on v3

--- a/solution.py
+++ b/solution.py
@@ -8,7 +8,8 @@
 K = 8192
 MESH = pl.DeviceIdType.MESH
 NX, NY, NZ, NC = 4, 4, 8, 2
-CH, RC, RZ, HP = 4, 64, 8, 2
+CH, RC, RZ, HP = 4, 64, 8, 1
+TJ = 2
 COLS, TILE = 512, 128
 
 
@@ -50,6 +51,18 @@
 
     own_cols = pl.ds(pl.multiple_of(c * half, half), half)
     sib_cols = pl.ds(pl.multiple_of(sib * half, half), half)
+    barrier = pltpu.get_barrier_semaphore()
+
+    def greet(where):
+        pl.semaphore_signal(barrier, inc=1, device_id=where, device_id_type=MESH)
+
+    for d in range(1, NZ):
+        greet(dev(x, y, (z + d) % NZ, c))
+    for dx in range(NX):
+        for dy in range(NY):
+            for cs in range(NC):
+                greet(dev((x + dx) % NX, (y + dy) % NY, z, cs))
+
     g_local = []
     for k in range(CH):
         g_local.append([
@@ -64,17 +77,6 @@
             copy.start()
     m_local.start()
 
-    barrier = pltpu.get_barrier_semaphore()
-
-    def greet(where):
-        pl.semaphore_signal(barrier, inc=1, device_id=where, device_id_type=MESH)
-
-    for dx in range(NX):
-        for dy in range(NY):
-            for cs in range(NC):
-                greet(dev((x + dx) % NX, (y + dy) % NY, z, cs))
-    for d in range(1, NZ):
-        greet(dev(x, y, (z + d) % NZ, c))
     pl.semaphore_wait(barrier, NX * NY * NC + NZ - 1)
 
     started = []
@@ -103,15 +105,15 @@
         ])
 
     own_sends(0)
-    trows = t_ref.shape[0] // HP
+    trows = t_ref.shape[0] // TJ
 
     def deal(j, cc):
         source = t_ref.at[pl.ds(j * trows, trows), pl.ds(cc * half, half)]
-        to = HP * c + j
+        to = TJ * c + j
         same = (to == y) & (cc == c)
         return same, remote(source, tb.at[y, z], ts.at[j, cc], tr, dev(x, to, z, cc)), source
 
-    for j in range(HP):
+    for j in range(TJ):
         for cc in range(NC):
             same, copy, source = deal(j, cc)
 
@@ -295,6 +297,16 @@
     z_sum(3)
     scores(2)
     scores(3)
+
+    for copy in started:
+        copy.wait_send()
+    for j in range(TJ):
+        for cc in range(NC):
+            same, copy, source = deal(j, cc)
+
+            @pl.when(jnp.logical_not(same))
+            def _():
+                copy.wait_send()
 
     for hh in range(2):
         arrived(fr.at[hh], ers.at[hh])
@@ -322,8 +334,6 @@
             * lax.rsqrt(m[RZ:RZ + 1] + 1e-06)
         )
 
-    for copy in started:
-        copy.wait_send()
     for k in range(CH):
         def leave(block):
             remote(block, block, es.at[k], es.at[k], dev(x, y, z, sib)).wait_send()
@@ -334,14 +344,6 @@
         @pl.when(c != k // 2)
         def _():
             leave(pb.at[k, 0, 0])
-    for j in range(HP):
-        for cc in range(NC):
-            same, copy, source = deal(j, cc)
-
-            @pl.when(jnp.logical_not(same))
-            def _():
-                copy.wait_send()
-
 
 def per_device(grads, proj_matrix, targets):
     depth, dims = proj_matrix.shape
@@ -365,13 +367,13 @@
             pltpu.VMEM((CH - 1, HP, NZ - 1, RZ, part), f32),
             pltpu.VMEM((HP, NZ - 1, RZ, part), bf16),
             pltpu.VMEM((CH, NY, RZ, half), f32),
-            pltpu.VMEM((NY, NZ, targets.shape[0] // HP, half), bf16),
+            pltpu.VMEM((NY, NZ, targets.shape[0] // TJ, half), bf16),
             pltpu.VMEM((COLS, COLS), bf16),
             pltpu.VMEM((CH, NY, NX, 2 * RZ, TILE), f32),
             pltpu.VMEM((2, NY, NX, NC, 2 * RZ, TILE), f32),
             dma((CH, NZ)), dma((2,)),
             dma((CH, 6)), dma((CH, 6)), dma((CH, 4)), dma((CH, 4)),
-            dma, dma, dma((HP, NC)), dma,
+            dma, dma, dma((TJ, NC)), dma,
             dma((NZ - 1,)), dma((NZ - 1,)),
             dma((CH, HP, NY - 1)), dma((CH, HP, NY - 1)),
             dma((CH, HP, NZ - 1)), dma((CH, HP, NZ - 1)),

time: 83 us -> 82.5 us (level)
  no operation moved by 1% of the time
where the time goes in v4:
time: 82.5 us; the launch traced here: 82.4 us
  Pallas kernels  81 us (98%)
  local copies, waits for them, and re-layouts  1.38 us (2%)
    pallas_call x1, Pallas kernels, per_device(): pl.pallas_call(kernel, out_shape=jax.ShapeDtypeStruct((2 * RZ, COLS), f32...  81 us

profile of v4, /device:TPU:1, one launch (start us, length us, event | category | flops | bytes accessed | tf_op | source)
XLA Modules:
  0.0 82.4 jit_solution(2611062316887320885)
XLA Ops:
  0.0 81.0 %shard_map.37 = f32[16,512]{1,0:T(8,128)} custom-call(bf16[256,2048]{1,0:T(8,128)(2,1)} %g_ref.1, bf16[2048,2048]{1,0:T(8,128)(2,1)} %m_ref.1, bf16[32,2048]{1,0:T(8,128)(2,1)} %t_ref.1), custom_call_target="tpu_custom_call" | custom-call | tf_op jit(solution)/shard_map/pallas_call | solution.py:354
  81.0 1.4 %copy.5 = f32[16,512]{1,0:T(8,128)} copy(f32[16,512]{1,0:T(8,128)} %shard_map.37) | data formatting | bytes 65536

commit v5 on v4

--- a/solution.py
+++ b/solution.py
@@ -172,7 +172,7 @@
         if k == CH - 1:
             zq[h] = total.astype(jnp.bfloat16)
             source = zq.at[h]
-        for d in range(1, NZ):
+        for d in (4, 3, 5, 2, 6, 1, 7):
             to = (z + d) % NZ
             piece = pl.ds(pl.multiple_of(to * RZ, RZ), RZ)
             go([remote(source.at[piece, :], z_slot(k, h, d),
@@ -228,6 +228,11 @@
             pb[k, :, b, 0:RZ, :] = both[:, b * TILE:(b + 1) * TILE].reshape(NY, RZ, TILE)
             for a in range(NY):
                 pb[k, a, b, RZ + 1:RZ + 2, 0:NY * RZ] = norms[0:1, :]
+        for dx in (2, 1, 3, 0):
+            for dy in (2, 1, 3, 0):
+                if dx or dy:
+                    owner_copy(k, dx, dy).start()
+
         same = c == k // 2
 
         @pl.when(same)
@@ -237,11 +242,6 @@
         @pl.when(jnp.logical_not(same))
         def _():
             owner_copy(k, 0, 0).start()
-
-        for dx in range(NX):
-            for dy in range(NY):
-                if dx or dy:
-                    owner_copy(k, dx, dy).start()
 
     def forward(k):
         arrived(rows_of(k, left, 0), gr.at[k, 0])

time: 82.5 us -> 82.3 us (level)
  no operation moved by 1% of the time
where the time goes in v5:
time: 82.3 us; the launch traced here: 82.2 us
  Pallas kernels  80.8 us (98%)
  local copies, waits for them, and re-layouts  1.38 us (2%)
    pallas_call x1, Pallas kernels, per_device(): pl.pallas_call(kernel, out_shape=jax.ShapeDtypeStruct((2 * RZ, COLS), f32...  80.8 us

profile of v5, /device:TPU:1, one launch (start us, length us, event | category | flops | bytes accessed | tf_op | source)
XLA Modules:
  0.0 82.2 jit_solution(2500125864312675717)
XLA Ops:
  0.0 80.8 %shard_map.37 = f32[16,512]{1,0:T(8,128)} custom-call(bf16[256,2048]{1,0:T(8,128)(2,1)} %g_ref.1, bf16[2048,2048]{1,0:T(8,128)(2,1)} %m_ref.1, bf16[32,2048]{1,0:T(8,128)(2,1)} %t_ref.1), custom_call_target="tpu_custom_call" | custom-call | tf_op jit(solution)/shard_map/pallas_call | solution.py:354
  80.8 1.4 %copy.5 = f32[16,512]{1,0:T(8,128)} copy(f32[16,512]{1,0:T(8,128)} %shard_map.37) | data formatting | bytes 65536
